TPU v7x, 32 devices: a whole 2x2x4 slice. The times are simulated.
32 devices in a mesh: rep: 8 (over z, y), shard: 4 (over x, core).
Axes of the slice: x: 2, y: 2, z: 4, core: 2. Of those that a mesh axis runs over, the one named last changes fastest.
Arguments:
- tokens: bfloat16 [8, 1024, 2304], P('rep', 'shard'), may hold values from -6 to 6
- cotangent: bfloat16 [8, 1024, 2304], P('rep', 'shard'), may hold values from -6 to 6
- sequence_adapter_index: int32 [8], P('rep'), may hold values from 0 to 7
- image_span_start: int32 [8, 2], P('rep'), may hold values from 0 to 768, as said below
- attention_norm_gain: bfloat16 [2304], replicated, may hold values from 0.099609375 to 1.8984375
- feedforward_norm_gain: bfloat16 [2304], replicated, may hold values from 0.099609375 to 1.8984375
- query_key_value_weight: bfloat16 [3, 2304, 2304], P(None, 'shard'), may hold values from -0.125 to 0.125
- attention_output_weight: bfloat16 [2304, 2304], P('shard'), may hold values from -2 to 2
- gate_up_projection_weight: bfloat16 [2, 2304, 5760], P(None, 'shard'), may hold values from -0.125 to 0.125
- down_projection_weight: bfloat16 [5760, 2304], P('shard'), may hold values from -0.625 to 0.625
- adapter_model_input_maps: bfloat16 [6, 8, 16, 2304], P(None, 'shard'), may hold values from -0.125 to 0.125
- adapter_model_output_maps: bfloat16 [5, 8, 16, 2304], P(None, 'shard'), may hold values from -1.5 to 1.5
- adapter_hidden_input_map: bfloat16 [8, 16, 5760], P('shard'), may hold values from -0.078125 to 0.078125
- adapter_hidden_output_maps: bfloat16 [2, 8, 16, 5760], P(None, 'shard'), may hold values from -1.5 to 1.5
Outputs:
- output: bfloat16 [8, 1024, 2304], P('rep', 'shard')
- input_grad: float32 [8, 1024, 2304], P('rep', 'shard')
- grad_a_model: float32 [6, 8, 16, 2304], P(None, 'shard')
- grad_b_model: float32 [5, 8, 16, 2304], P(None, 'shard')
- grad_a_hidden: float32 [8, 16, 5760], P('shard')
- grad_b_hidden: float32 [2, 8, 16, 5760], P(None, 'shard')
Inputs may be any that keep to these rules, and one draw needn't show every extreme that they name: `image_span_start`: in each sequence the first span starts in 0 to 256 and the second in 512 to 768; some sequence's first span starts at 0 and some sequence's second span ends at the sequence's end.
All inputs are finite; a program needn't handle non-finite values.
Results may differ from a plain program's by a relative error of at most 0.023.
Values may be sent and summed in bfloat16 or wider, within the bound.
No kernel may reach another device: no remote copies, remote signals or barrier semaphores. Data moves between devices by JAX's collectives and lax.ppermute only.
A program may use at most 512 MiB of HBM per device.

v0:
```python
import math
import jax
import jax.numpy as jnp
from jax import lax
from jax.sharding import PartitionSpec as P

HDIM = 64
SPAN = 256
EPS = 1e-05
THETA = 10000.0
BRANCH = 1.4 / math.sqrt(40.0)


def norm_rows(values, gain):
    return values * lax.rsqrt(jnp.mean(values * values, axis=-1, keepdims=True) + EPS) * gain


def rotate(values, positions):
    rows = values.shape[0]
    heads = values.shape[1] // HDIM
    half = HDIM // 2
    exponent = jnp.arange(half, dtype=jnp.float32) * (-2.0 / HDIM)
    frequency = jnp.exp(exponent * math.log(THETA))
    angle = positions.astype(jnp.float32)[:, None] * frequency[None, :]
    cosine = jnp.concatenate([jnp.cos(angle), jnp.cos(angle)], axis=1)[:, None, :]
    sine = jnp.concatenate([jnp.sin(angle), jnp.sin(angle)], axis=1)[:, None, :]
    split = values.reshape(rows, heads, HDIM)
    turned = jnp.concatenate([-split[..., half:], split[..., :half]], axis=-1)
    return (split * cosine + turned * sine).reshape(rows, heads * HDIM)


def span_label(positions, starts):
    label = jnp.full(positions.shape, -1, jnp.int32)
    for number in range(starts.shape[0]):
        inside = (positions >= starts[number]) & (positions < starts[number] + SPAN)
        label = jnp.where(inside, jnp.int32(number), label)
    return label


def visible_pairs(rows, columns, starts):
    row_label = span_label(rows, starts)[:, None]
    column_label = span_label(columns, starts)[None, :]
    causal = columns[None, :] <= rows[:, None]
    return causal | (row_label == column_label) & (row_label >= 0)


def rounded_amount(values):
    return lax.optimization_barrier(values.astype(jnp.bfloat16)).astype(jnp.float32)


def heads_of(values):
    return values.reshape(values.shape[0], values.shape[1] // HDIM, HDIM)


def attention_scores(queries, keys, visible):
    raw = jnp.einsum(
        "qhd,khd->hqk", heads_of(queries), heads_of(keys), preferred_element_type=jnp.float32
    )
    return jnp.where(visible[None], raw * (1.0 / math.sqrt(HDIM)), -1e30)


def shards(
    tokens,
    cotangent,
    sequence_adapter_index,
    image_span_start,
    attention_norm_gain,
    feedforward_norm_gain,
    query_key_value_weight,
    attention_output_weight,
    gate_up_projection_weight,
    down_projection_weight,
    adapter_model_input_maps,
    adapter_model_output_maps,
    adapter_hidden_input_map,
    adapter_hidden_output_maps,
):
    local_rows = tokens.shape[1]
    width = tokens.shape[2]
    group = lax.axis_size("shard")
    place = lax.axis_index("shard")
    pick = sequence_adapter_index[0]
    starts = image_span_start[0]
    positions_local = place * local_rows + jnp.arange(local_rows, dtype=jnp.int32)
    positions_all = jnp.arange(local_rows * group, dtype=jnp.int32)
    visible = visible_pairs(positions_local, positions_all, starts)
    residual_in = tokens[0].astype(jnp.float32)
    gain_one = attention_norm_gain.astype(jnp.float32)
    gain_two = feedforward_norm_gain.astype(jnp.float32)
    a_model_all, b_model_all, a_hidden_all, b_hidden_all = (
        lax.all_gather(adapter_model_input_maps, "shard", axis=1, tiled=True),
        lax.all_gather(adapter_model_output_maps, "shard", axis=1, tiled=True),
        lax.all_gather(adapter_hidden_input_map[None], "shard", axis=1, tiled=True),
        lax.all_gather(adapter_hidden_output_maps, "shard", axis=1, tiled=True),
    )
    a_one = lax.dynamic_index_in_dim(a_model_all, pick, 1, keepdims=False)
    b_one = lax.dynamic_index_in_dim(b_model_all, pick, 1, keepdims=False)
    single_hidden_input_map = lax.dynamic_index_in_dim(a_hidden_all, pick, 1, keepdims=False)[0]
    b_hidden_one = lax.dynamic_index_in_dim(b_hidden_all, pick, 1, keepdims=False)
    normed = norm_rows(residual_in, gain_one).astype(jnp.bfloat16)
    empty = jnp.zeros((local_rows, width), jnp.float32)
    pieces = lax.all_gather(query_key_value_weight, "shard", axis=1, tiled=True)
    columns = normed
    base_query, base_key, base_value = tuple(
        (jnp.dot(columns, pieces[slot], preferred_element_type=jnp.float32) for slot in range(3))
    )
    narrow_first = jnp.einsum(
        "td,srd->str", normed, a_one[0:3], preferred_element_type=jnp.float32
    ).astype(jnp.bfloat16)
    lifted_first = jnp.einsum(
        "str,srd->std", narrow_first, b_one[0:3], preferred_element_type=jnp.float32
    )
    query = base_query + lifted_first[0]
    key_pre = base_key + lifted_first[1]
    value_low = (base_value + lifted_first[2]).astype(jnp.bfloat16)
    query_turned = rotate(query, positions_local).astype(jnp.bfloat16)
    key_turned = rotate(key_pre, positions_local).astype(jnp.bfloat16)
    keys_all, values_all = (
        lax.all_gather(key_turned, "shard", axis=0, tiled=True),
        lax.all_gather(value_low, "shard", axis=0, tiled=True),
    )
    scores = attention_scores(query_turned, keys_all, visible)
    top = jnp.max(scores, axis=-1, keepdims=True)
    weights = jnp.exp(scores - top)
    total = jnp.sum(weights, axis=-1, keepdims=True)
    log_total = top + jnp.log(total)
    probs = weights / total
    mixed = jnp.einsum(
        "hqk,khd->qhd",
        probs.astype(jnp.bfloat16),
        heads_of(values_all),
        preferred_element_type=jnp.float32,
    )
    mixed_low = mixed.reshape(local_rows, width).astype(jnp.bfloat16)
    columns = mixed_low
    base_out = jnp.dot(
        columns,
        lax.all_gather(attention_output_weight, "shard", axis=0, tiled=True),
        preferred_element_type=jnp.float32,
    )
    narrow_out = jnp.einsum(
        "td,rd->tr", mixed_low, a_one[3], preferred_element_type=jnp.float32
    ).astype(jnp.bfloat16)
    branch = base_out + jnp.dot(narrow_out, b_one[3], preferred_element_type=jnp.float32)
    middle = residual_in + BRANCH * branch
    normed_second = norm_rows(middle, gain_two).astype(jnp.bfloat16)
    narrow_mlp = jnp.einsum(
        "td,srd->str", normed_second, a_one[4:6], preferred_element_type=jnp.float32
    ).astype(jnp.bfloat16)
    lifted_mlp = jnp.einsum(
        "str,srf->stf", narrow_mlp, b_hidden_one, preferred_element_type=jnp.float32
    )
    columns = normed_second
    base_gate_up = jnp.einsum(
        "tr,srf->stf",
        columns,
        lax.all_gather(gate_up_projection_weight, "shard", axis=1, tiled=True),
        preferred_element_type=jnp.float32,
    )
    gate = base_gate_up[0] + lifted_mlp[0]
    up = base_gate_up[1] + lifted_mlp[1]
    hidden_low = (jax.nn.silu(gate) * up).astype(jnp.bfloat16)
    narrow_down = jnp.einsum(
        "tf,rf->tr", hidden_low, single_hidden_input_map, preferred_element_type=jnp.float32
    ).astype(jnp.bfloat16)
    columns = hidden_low
    base_down = jnp.dot(
        columns,
        lax.all_gather(down_projection_weight, "shard", axis=0, tiled=True),
        preferred_element_type=jnp.float32,
    )
    feed = base_down + jnp.dot(narrow_down, b_one[4], preferred_element_type=jnp.float32)
    output = (middle + BRANCH * feed).astype(jnp.bfloat16)
    grad_out = cotangent[0].astype(jnp.float32)
    grad_feed = (BRANCH * grad_out).astype(jnp.bfloat16)
    grad_b_down = jnp.einsum(
        "tr,td->rd", narrow_down, grad_feed, preferred_element_type=jnp.float32
    )
    down_lowrank_gradient = jnp.einsum(
        "td,rd->tr", grad_feed, b_one[4], preferred_element_type=jnp.float32
    ).astype(jnp.bfloat16)
    grad_a_down = jnp.einsum(
        "tr,tf->rf", down_lowrank_gradient, hidden_low, preferred_element_type=jnp.float32
    )
    adapter_hidden_output = jnp.dot(
        down_lowrank_gradient, single_hidden_input_map, preferred_element_type=jnp.float32
    )
    frozen_hidden_output = jnp.einsum(
        "td,rd->tr",
        grad_feed,
        lax.all_gather(down_projection_weight, "shard", axis=0, tiled=True),
        preferred_element_type=jnp.float32,
    )
    hidden_gradient = rounded_amount(frozen_hidden_output + adapter_hidden_output)
    _, silu_back = jax.vjp(lambda gate_in, up_in: jax.nn.silu(gate_in) * up_in, gate, up)
    grad_gate, grad_up = silu_back(hidden_gradient)
    stacked_mlp = jnp.stack([grad_gate.astype(jnp.bfloat16), grad_up.astype(jnp.bfloat16)])
    grad_b_mlp = jnp.einsum(
        "str,stf->srf", narrow_mlp, stacked_mlp, preferred_element_type=jnp.float32
    )
    grad_narrow_mlp = jnp.einsum(
        "stf,srf->str", stacked_mlp, b_hidden_one, preferred_element_type=jnp.float32
    ).astype(jnp.bfloat16)
    grad_a_mlp = jnp.einsum(
        "str,td->srd", grad_narrow_mlp, normed_second, preferred_element_type=jnp.float32
    )
    adapter_second_output = jnp.einsum(
        "str,srd->td", grad_narrow_mlp, a_one[4:6], preferred_element_type=jnp.float32
    )
    frozen_second_output = jnp.einsum(
        "stf,srf->tr",
        stacked_mlp,
        lax.all_gather(gate_up_projection_weight, "shard", axis=1, tiled=True),
        preferred_element_type=jnp.float32,
    )
    second_normed_gradient = frozen_second_output + adapter_second_output
    _, norm_back_second = jax.vjp(lambda values: norm_rows(values, gain_two), middle)
    grad_middle = grad_out + norm_back_second(second_normed_gradient)[0]
    grad_branch = (BRANCH * grad_middle).astype(jnp.bfloat16)
    grad_b_out = jnp.einsum(
        "tr,td->rd", narrow_out, grad_branch, preferred_element_type=jnp.float32
    )
    grad_narrow_out = jnp.einsum(
        "td,rd->tr", grad_branch, b_one[3], preferred_element_type=jnp.float32
    ).astype(jnp.bfloat16)
    grad_a_out = jnp.einsum(
        "tr,td->rd", grad_narrow_out, mixed_low, preferred_element_type=jnp.float32
    )
    base_mixed = jnp.einsum(
        "td,rd->tr",
        grad_branch,
        lax.all_gather(attention_output_weight, "shard", axis=0, tiled=True),
        preferred_element_type=jnp.float32,
    )
    grad_mixed = (
        base_mixed + jnp.dot(grad_narrow_out, a_one[3], preferred_element_type=jnp.float32)
    ).astype(jnp.bfloat16)
    probs_again = jnp.exp(attention_scores(query_turned, keys_all, visible) - log_total)
    grad_mixed_heads = heads_of(grad_mixed)
    grad_probs = jnp.einsum(
        "qhd,khd->hqk", grad_mixed_heads, heads_of(values_all), preferred_element_type=jnp.float32
    )
    inner = jnp.sum(grad_probs * probs_again, axis=-1, keepdims=True)
    grad_scores = (probs_again * (grad_probs - inner)).astype(jnp.bfloat16)
    scale = 1.0 / math.sqrt(HDIM)
    grad_query_turned = (
        jnp.einsum(
            "hqk,khd->qhd", grad_scores, heads_of(keys_all), preferred_element_type=jnp.float32
        ).reshape(local_rows, width)
        * scale
    )
    key_terms = (
        jnp.einsum(
            "hqk,qhd->khd", grad_scores, heads_of(query_turned), preferred_element_type=jnp.float32
        ).reshape(keys_all.shape[0], width)
        * scale
    )
    value_terms = jnp.einsum(
        "hqk,qhd->khd",
        probs_again.astype(jnp.bfloat16),
        grad_mixed_heads,
        preferred_element_type=jnp.float32,
    ).reshape(keys_all.shape[0], width)
    grad_key_turned, grad_value = (
        lax.psum_scatter(
            key_terms.astype(jnp.bfloat16), "shard", scatter_dimension=0, tiled=True
        ).astype(jnp.float32),
        lax.psum_scatter(
            value_terms.astype(jnp.bfloat16), "shard", scatter_dimension=0, tiled=True
        ).astype(jnp.float32),
    )
    _, turn_back = jax.vjp(lambda values: rotate(values, positions_local), empty)
    stacked_first = jnp.stack(
        [
            turn_back(grad_query_turned)[0].astype(jnp.bfloat16),
            turn_back(grad_key_turned)[0].astype(jnp.bfloat16),
            grad_value.astype(jnp.bfloat16),
        ]
    )
    grad_b_first = jnp.einsum(
        "str,std->srd", narrow_first, stacked_first, preferred_element_type=jnp.float32
    )
    grad_narrow_first = jnp.einsum(
        "std,srd->str", stacked_first, b_one[0:3], preferred_element_type=jnp.float32
    ).astype(jnp.bfloat16)
    grad_a_first = jnp.einsum(
        "str,td->srd", grad_narrow_first, normed, preferred_element_type=jnp.float32
    )
    base_normed = jnp.einsum(
        "std,srd->tr",
        stacked_first,
        lax.all_gather(query_key_value_weight, "shard", axis=1, tiled=True),
        preferred_element_type=jnp.float32,
    )
    grad_normed = base_normed + jnp.einsum(
        "str,srd->td", grad_narrow_first, a_one[0:3], preferred_element_type=jnp.float32
    )
    _, norm_back_first = jax.vjp(lambda values: norm_rows(values, gain_one), residual_in)
    input_grad = grad_middle + norm_back_first(grad_normed)[0]
    grad_a_model_one = jnp.concatenate([grad_a_first, grad_a_out[None], grad_a_mlp], axis=0)
    grad_b_model_one = jnp.concatenate([grad_b_first, grad_b_out[None], grad_b_down[None]], axis=0)
    per_processor_share = adapter_model_input_maps.shape[1]
    adapters_total = per_processor_share * group
    chosen = (jnp.arange(adapters_total, dtype=jnp.int32) == pick).astype(jnp.float32)[
        None, :, None, None
    ]
    spread_a_model = grad_a_model_one[:, None] * chosen
    spread_b_model = grad_b_model_one[:, None] * chosen
    spread_a_hidden = grad_a_down[None, None] * chosen
    spread_b_hidden = grad_b_mlp[:, None] * chosen
    owned = (
        lax.psum_scatter(
            spread_a_model.astype(jnp.bfloat16), "shard", scatter_dimension=1, tiled=True
        ).astype(jnp.float32),
        lax.psum_scatter(
            spread_b_model.astype(jnp.bfloat16), "shard", scatter_dimension=1, tiled=True
        ).astype(jnp.float32),
        lax.psum_scatter(
            spread_a_hidden.astype(jnp.bfloat16), "shard", scatter_dimension=1, tiled=True
        ).astype(jnp.float32),
        lax.psum_scatter(
            spread_b_hidden.astype(jnp.bfloat16), "shard", scatter_dimension=1, tiled=True
        ).astype(jnp.float32),
    )
    summed = (
        lax.psum(owned[0].astype(jnp.bfloat16), "rep").astype(jnp.float32),
        lax.psum(owned[1].astype(jnp.bfloat16), "rep").astype(jnp.float32),
        lax.psum(owned[2].astype(jnp.bfloat16), "rep").astype(jnp.float32),
        lax.psum(owned[3].astype(jnp.bfloat16), "rep").astype(jnp.float32),
    )
    return (output[None], input_grad[None], summed[0], summed[1], summed[2][0], summed[3])


def solution(mesh):
    in_specs = (
        P("rep", "shard", None),
        P("rep", "shard", None),
        P("rep"),
        P("rep", None),
        P(),
        P(),
        P(None, "shard", None),
        P("shard", None),
        P(None, "shard", None),
        P("shard", None),
        P(None, "shard", None, None),
        P(None, "shard", None, None),
        P("shard", None, None),
        P(None, "shard", None, None),
    )
    out_specs = (
        P("rep", "shard", None),
        P("rep", "shard", None),
        P(None, "shard", None, None),
        P(None, "shard", None, None),
        P("shard", None, None),
        P(None, "shard", None, None),
    )
    return jax.shard_map(shards, mesh=mesh, in_specs=in_specs, out_specs=out_specs, check_vma=False)
```

profile of v0, /device:TPU:0, one launch (start us, length us, event | category | flops | bytes accessed | tf_op | source)
XLA Modules:
  0.0 1554.4 jit_solution(16283073855144799213)
XLA Ops:
  14.0 29.6 %all-gather.14.cloned.1.call-done = bf16[6,8,16,2304]{3,2,0,1:T(8,128)(2,1)} async-done(((bf16[6,2,16,2304]{3,2,0,1:T(8,128)(2,1)}), bf16[6,8,16,2304]{3,2,0,1:T(8,128)(2,1)}) %all-gather.14.cloned.1.call-update) | async-done | bytes 3538960 | tf_op jit(solution)/shard_map/all_gather | solution.py:91
  45.1 28.1 %all-gather.16.cloned.1.call-done = bf16[5,8,16,2304]{3,2,0,1:T(8,128)(2,1)} async-done(((bf16[5,2,16,2304]{3,2,0,1:T(8,128)(2,1)}), bf16[5,8,16,2304]{3,2,0,1:T(8,128)(2,1)}) %all-gather.16.cloned.1.call-update) | async-done | bytes 2949136 | tf_op jit(solution)/shard_map/all_gather | solution.py:92
  78.2 188.6 %all-gather.12.cloned.1.call-done = bf16[3,2304,2304]{2,1,0:T(8,128)(2,1)} async-done(((bf16[3,576,2304]{2,1,0:T(8,128)(2,1)}), bf16[3,2304,2304]{2,1,0:T(8,128)(2,1)}) %all-gather.12.cloned.1.call-update) | async-done | bytes 31850512 | tf_op jit(solution)/shard_map/all_gather | solution.py:102
  335.1 95.6 %all-gather.28.cloned.1.call-done = bf16[5760,2304]{1,0:T(8,128)(2,1)} async-done(((bf16[1440,2304]{1,0:T(8,128)(2,1)}), bf16[5760,2304]{1,0:T(8,128)(2,1)}) %all-gather.28.cloned.1.call-update) | async-done | bytes 26542096 | tf_op jit(solution)/shard_map/all_gather | solution.py:169
  430.7 15.2 fusion.93
  457.2 33.5 %all-gather.18.cloned.1.call-done = bf16[1024,2304]{1,0:T(8,128)(2,1)} async-done(((bf16[256,2304]{1,0:T(8,128)(2,1)}), bf16[1024,2304]{1,0:T(8,128)(2,1)}) %all-gather.18.cloned.1.call-update) | async-done | bytes 4718608 | tf_op jit(solution)/shard_map/all_gather | solution.py:120
  497.3 33.0 %all-gather.20.cloned.1.call-done = bf16[1024,2304]{1,0:T(8,128)(2,1)} async-done(((bf16[256,2304]{1,0:T(8,128)(2,1)}), bf16[1024,2304]{1,0:T(8,128)(2,1)}) %all-gather.20.cloned.1.call-update) | async-done | bytes 4718608 | tf_op jit(solution)/shard_map/all_gather | solution.py:119
  536.9 19.5 %fusion.6 = (f32[36,256]{1,0:T(8,128)S(1)}, f32[36,256,1024]{2,1,0:T(8,128)}) fusion(pred[256,1024]{1,0:T(8,128)(4,1)S(1)} %fusion.91, bf16[256,36,64]{0,2,1:T(8,128)(2,1)S(1)} %bitcast.303, bf16[1024,36,64]{0,2,1:T(8,128)(2,1)} %bitcast.298), kind=kOutput, calls=%fused_computation.11 | convolution fusion | flops 1236261888 | bytes 43945984 | tf_op jit(solution)/shard_map/qhd,khd->hqk/dot_general | solution.py:56
  556.4 17.5 %fusion = f32[36,256]{1,0:T(8,128)S(1)} fusion(f32[36,256]{1,0:T(8,128)S(1)} %get-tuple-element.39, f32[36,256,1024]{2,1,0:T(8,128)} %get-tuple-element.40, pred[256,1024]{1,0:T(8,128)(4,1)S(1)} %fusion.91), kind=kLoop, calls=%fused_computation.6 | loop fusion | flops 37739520 | bytes 38084608 | tf_op jit(solution)/shard_map/reduce_sum | solution.py:125
  574.0 15.9 %fusion.65 = bf16[36,64,256]{2,1,0:T(8,128)(2,1)S(1)} fusion(bf16[1024,36,64]{0,2,1:T(8,128)(2,1)S(1)} %bitcast.301, f32[36,256]{1,0:T(8,128)S(1)} %fusion, f32[36,256]{1,0:T(8,128)S(1)} %get-tuple-element.39, f32[36,256,1024]{2,1,0:T(8,128)} %get-tuple-element.40, pred[256,1024]{1,0:T(8,128)(4,1)S(1)} %fusion.91), kind=kOutput, calls=%fused_computation.121 | convolution fusion | flops 1255735296 | bytes 43982848 | tf_op jit(solution)/shard_map/hqk,khd->qhd/dot_general | solution.py:128
  614.0 17.9 %all-gather.26.cloned.1.call-done = bf16[2,8,16,5760]{3,2,1,0:T(8,128)(2,1)} async-done(((bf16[2,2,16,5760]{3,2,1,0:T(8,128)(2,1)}), bf16[2,8,16,5760]{3,2,1,0:T(8,128)(2,1)}) %all-gather.26.cloned.1.call-update) | async-done | bytes 2949136 | tf_op jit(solution)/shard_map/all_gather | solution.py:94
  638.9 308.1 %all-gather.24.cloned.1.call-done = bf16[2,2304,5760]{2,1,0:T(8,128)(2,1)} async-done(((bf16[2,576,5760]{2,1,0:T(8,128)(2,1)}), bf16[2,2304,5760]{2,1,0:T(8,128)(2,1)}) %all-gather.24.cloned.1.call-update) | async-done | bytes 53084176 | tf_op jit(solution)/shard_map/all_gather | solution.py:157
  947.0 26.5 %convolution_bitcast_fusion = f32[2,256,5760]{2,1,0:T(8,128)} fusion(bf16[256,2304,1]{1,0,2:T(8,128)(2,1)S(1)} %fusion.66, bf16[2,2304,5760]{2,1,0:T(8,128)(2,1)} %all-gather.24.cloned.1.call-done), kind=kOutput, calls=%fused_computation.18 | convolution fusion | flops 13589544960 | bytes 66060288 | tf_op jit(solution)/shard_map/tr,srf->stf/dot_general | solution.py:154
  973.5 13.2 fusion.43
  995.1 24.0 %convolution_bitcast_fusion.2 = f32[256,2304]{1,0:T(8,128)} fusion(bf16[2,2304,5760]{2,1,0:T(8,128)(2,1)} %all-gather.24.cloned.1.call-done, bf16[1,256,5760]{2,1,0:T(8,128)(2,1)} %get-tuple-element.17, bf16[1,256,5760]{2,1,0:T(8,128)(2,1)} %get-tuple-element.13), kind=kOutput, calls=%fused_computation.55 | convolution fusion | flops 13592494080 | bytes 61341696 | tf_op jit(solution)/shard_map/stf,srf->tr/dot_general | solution.py:210
  1033.3 29.5 %multiply_reduce_fusion = (f32[36,256]{1,0:T(8,128)S(1)}, f32[36,256,1024]{2,1,0:T(8,128)}) fusion(f32[36,256]{1,0:T(8,128)S(1)} %copy-done.34, f32[36,256,1024]{2,1,0:T(8,128)} %get-tuple-element.40, pred[256,1024]{1,0:T(8,128)(4,1)S(1)} %copy-done.18, bf16[256,36,64]{0,2,1:T(8,128)(2,1)S(1)} %bitcast.315, bf16[1024,36,64]{0,2,1:T(8,128)(2,1)} %bitcast.300), kind=kOutput, calls=%fused_computation.1 | convolution fusion | flops 1255136256 | bytes 81731584 | tf_op jit(solution)/shard_map/qhd,khd->hqk/dot_general | solution.py:240
  1062.8 31.5 %multiply_convert_fusion = bf16[36,256,1024]{2,1,0:T(8,128)(2,1)} fusion(f32[36,256,1024]{2,1,0:T(8,128)} %get-tuple-element.46, f32[36,256]{1,0:T(8,128)S(1)} %get-tuple-element.45, f32[36,256]{1,0:T(8,128)S(1)} %copy-done.34, f32[36,256,1024]{2,1,0:T(8,128)} %get-tuple-element.40, pred[256,1024]{1,0:T(8,128)(4,1)S(1)} %copy-done.18), kind=kLoop, calls=%fused_computation | loop fusion | flops 56623104 | bytes 94707712 | tf_op jit(solution)/shard_map/convert_element_type | solution.py:244
  1106.4 21.0 %fusion.44 = bf16[36,64,1024]{2,1,0:T(8,128)(2,1)} fusion(bf16[256,36,64]{0,2,1:T(8,128)(2,1)S(1)} %bitcast.316, f32[36,256]{1,0:T(8,128)S(1)} %copy-done.34, f32[36,256,1024]{2,1,0:T(8,128)} %get-tuple-element.40, pred[256,1024]{1,0:T(8,128)(4,1)S(1)} %copy-done.18), kind=kOutput, calls=%fused_computation.89 | convolution fusion | flops 1248067584 | bytes 43945984 | tf_op jit(solution)/shard_map/hqk,qhd->khd/dot_general | solution.py:258
  1168.7 36.1 %reduce-scatter.15.cloned.1.call-done = bf16[256,2304]{1,0:T(8,128)(2,1)} async-done(((bf16[1024,2304]{1,0:T(8,128)(2,1)}), bf16[256,2304]{1,0:T(8,128)(2,1)}) %reduce-scatter.15.cloned.1.call-update) | async-done | bytes 1179664 | tf_op jit(solution)/shard_map/reduce_scatter | solution.py:268
  1220.5 13.7 fusion.147
  1236.6 148.9 %all-reduce.14.cloned.1.call-done = (bf16[6,8,16,2304]{3,2,1,0:T(8,128)(2,1)}, bf16[5,8,16,2304]{3,2,1,0:T(8,128)(2,1)}, bf16[2,8,16,5760]{3,2,1,0:T(8,128)(2,1)}) async-done(((bf16[6,8,16,2304]{3,2,1,0:T(8,128)(2,1)}, bf16[5,8,16,2304]{3,2,1,0:T(8,128)(2,1)}, bf16[2,8,16,5760]{3,2,1,0:T(8,128)(2,1)}), (bf16[6,8,16,2304]{3,2,1,0:T(8,128)(2,1)}, bf16[5,8,16,2304]{3,2,1,0:T(8,128)(2,1)}, ...) | async-done | bytes 9437200
  1391.9 24.4 %reduce-scatter.17.cloned.1.call-done = bf16[1,2,16,5760]{3,2,1,0:T(8,128)(2,1)} async-done(((bf16[1,8,16,5760]{3,2,1,0:T(8,128)(2,1)}), bf16[1,2,16,5760]{3,2,1,0:T(8,128)(2,1)}) %reduce-scatter.17.cloned.1.call-update) | async-done | bytes 368656 | tf_op jit(solution)/shard_map/reduce_scatter | solution.py:318
  1416.3 15.4 convolution_bitcast_fusion.1
  1435.5 105.1 %all-reduce.12.cloned.1.call-done = (bf16[6,2,16,2304]{3,2,1,0:T(8,128)(2,1)}, bf16[5,2,16,2304]{3,2,1,0:T(8,128)(2,1)}, bf16[2,16,5760]{2,1,0:T(8,128)(2,1)}, bf16[2,2,16,5760]{3,2,1,0:T(8,128)(2,1)}) async-done(((bf16[6,2,16,2304]{3,2,1,0:T(8,128)(2,1)}, bf16[5,2,16,2304]{3,2,1,0:T(8,128)(2,1)}, bf16[2,16,5760]{2,1,0:T(8,128)(2,1)}, bf16[2,2,16,5760]{3,2,1,0:T(8,128)(2,1)}), ...) | async-done | bytes 2727952 | tf_op jit(solution)/shard_map/psum | solution.py:326
  (278 shorter events, 244.9 us)
Async XLA Ops:
  7.2 36.5 %all-gather.14.cloned.1.call-start = ((), (), s32[]{:S(2)}) async-start(), calls=%async_computation.4 | async-start | bytes 4423680 | tf_op jit(solution)/shard_map/all_gather | solution.py:91
  9.4 63.8 %all-gather.16.cloned.1.call-start = ((), (), s32[]{:S(2)}) async-start(), calls=%async_computation.5 | async-start | bytes 3686400 | tf_op jit(solution)/shard_map/all_gather | solution.py:92
  10.4 256.3 %all-gather.12.cloned.1.call-start = ((), (), s32[]{:S(2)}) async-start(), calls=%async_computation.3 | async-start | bytes 39813120 | tf_op jit(solution)/shard_map/all_gather | solution.py:102
  11.2 419.5 %all-gather.28.cloned.1.call-start = ((), (), s32[]{:S(2)}) async-start(), calls=%async_computation.11 | async-start | bytes 33177600 | tf_op jit(solution)/shard_map/all_gather | solution.py:169
  11.8 439.4 %all-gather.30.cloned.1.call-start = ((), (), s32[]{:S(2)}) async-start(), calls=%async_computation.15 | async-start | bytes 1843200 | tf_op jit(solution)/shard_map/all_gather | solution.py:93
  12.4 478.3 %all-gather.18.cloned.1.call-start = ((), (), s32[]{:S(2)}) async-start(), calls=%async_computation.6 | async-start | bytes 5898240 | tf_op jit(solution)/shard_map/all_gather | solution.py:120
  13.1 282.9 %copy-start.53 = (f32[2304]{0:T(1024)}, f32[2304]{0:T(1024)S(1)}, u32[]{:S(2)}) copy-start(f32[2304]{0:T(1024)S(1)} %convert_element_type.235) | copy-start | bytes 27652
  14.0 281.9 %copy-start.68 = (f32[256]{0:T(256)}, f32[256]{0:T(256)S(1)}, u32[]{:S(2)}) copy-start(f32[256]{0:T(256)S(1)} %fusion.123) | copy-start | bytes 3076
  275.5 254.9 %all-gather.20.cloned.1.call-start = ((), (), s32[]{:S(2)}) async-start(), calls=%async_computation.7 | async-start | bytes 5898240 | tf_op jit(solution)/shard_map/all_gather | solution.py:119
  326.1 276.7 %all-gather.22.cloned.1.call-start = ((), (), s32[]{:S(2)}) async-start(), calls=%async_computation.8 | async-start | bytes 13271040 | tf_op jit(solution)/shard_map/all_gather | solution.py:138
  326.9 305.0 %all-gather.26.cloned.1.call-start = ((), (), s32[]{:S(2)}) async-start(), calls=%async_computation.10 | async-start | bytes 3686400 | tf_op jit(solution)/shard_map/all_gather | solution.py:94
  327.7 619.3 %all-gather.24.cloned.1.call-start = ((), (), s32[]{:S(2)}) async-start(), calls=%async_computation.9 | async-start | bytes 66355200 | tf_op jit(solution)/shard_map/all_gather | solution.py:157
  328.3 835.9 %reduce-scatter.13.cloned.1.call-start = ((), (), s32[]{:S(2)}) async-start(), calls=%async_computation.12 | async-start | bytes 5898240 | tf_op jit(solution)/shard_map/reduce_scatter | solution.py:265
  333.7 240.3 %copy-start.17 = (pred[256,1024]{1,0:T(8,128)(4,1)}, pred[256,1024]{1,0:T(8,128)(4,1)S(1)}, u32[]{:S(2)}) copy-start(pred[256,1024]{1,0:T(8,128)(4,1)S(1)} %fusion.91) | copy-start | bytes 786436
  335.1 116.1 %copy-start.55 = (bf16[256,16]{0,1:T(8,128)(2,1)}, bf16[256,16]{0,1:T(8,128)(2,1)S(1)}, u32[]{:S(2)}) copy-start(bf16[256,16]{0,1:T(8,128)(2,1)S(1)} %fusion.85) | copy-start | bytes 24580
  457.2 79.8 %copy-start.8 = (bf16[256,2304]{0,1:T(8,128)(2,1)}, bf16[256,2304]{0,1:T(8,128)(2,1)S(1)}, u32[]{:S(2)}) copy-start(bf16[256,2304]{0,1:T(8,128)(2,1)S(1)} %copy.56) | copy-start | bytes 3538948
  610.7 414.6 %copy-start.1 = (f32[256,2304]{1,0:T(8,128)}, f32[256,2304]{1,0:T(8,128)S(1)}, u32[]{:S(2)}) copy-start(f32[256,2304]{1,0:T(8,128)S(1)} %get-tuple-element.42) | copy-start | bytes 7077892
  611.7 335.3 %copy-start.13 = (bf16[256,2304,1]{1,0,2:T(8,128)(2,1)}, bf16[256,2304,1]{1,0,2:T(8,128)(2,1)S(1)}, u32[]{:S(2)}) copy-start(bf16[256,2304,1]{1,0,2:T(8,128)(2,1)S(1)} %fusion.66) | copy-start | bytes 3538948
  1106.3 98.5 %reduce-scatter.15.cloned.1.call-start = ((), (), s32[]{:S(2)}) async-start(), calls=%async_computation.13 | async-start | bytes 5898240 | tf_op jit(solution)/shard_map/reduce_scatter | solution.py:268
  1134.1 251.5 %all-reduce.14.cloned.1.call-start = ((), (), s32[]{:S(2)}) async-start(), calls=%async_computation.17 | async-start | bytes 18874368
  1148.7 56.1 %copy-start.27 = (bf16[1,256,2304]{2,1,0:T(8,128)(2,1)}, bf16[1,256,2304]{2,1,0:T(8,128)(2,1)S(1)}, u32[]{:S(2)}) copy-start(bf16[1,256,2304]{2,1,0:T(8,128)(2,1)S(1)} %copy.63) | copy-start | bytes 3538948
  1168.7 38.2 %copy-start.29 = (bf16[1,256,2304]{2,1,0:T(8,128)(2,1)}, bf16[1,256,2304]{2,1,0:T(8,128)(2,1)S(1)}, u32[]{:S(2)}) copy-start(bf16[1,256,2304]{2,1,0:T(8,128)(2,1)S(1)} %copy.64) | copy-start | bytes 3538948
  1214.8 201.4 %reduce-scatter.17.cloned.1.call-start = ((), (), s32[]{:S(2)}) async-start(), calls=%async_computation.14 | async-start | bytes 1843200 | tf_op jit(solution)/shard_map/reduce_scatter | solution.py:318
  1220.4 320.2 %all-reduce.12.cloned.1.call-start = ((), (), s32[]{:S(2)}) async-start(), calls=%async_computation.16 | async-start | bytes 5455872 | tf_op jit(solution)/shard_map/psum | solution.py:326
  (68 other events, 458.1 us)
Sparse Core Ops, SparseCore 0:
  10.1 33.4 all-gather.13
  45.8 27.4 all-gather.15
  74.8 191.9 all-gather.11
  268.2 162.4 all-gather.27
  432.1 19.0 all-gather.29
  453.2 37.4 all-gather.17
  492.8 37.4 all-gather.19
  531.9 70.9 all-gather.21
  604.4 27.4 all-gather.25
  633.3 313.6 all-gather.23
  1106.4 47.8 reduce-scatter.12
  1156.9 47.8 reduce-scatter.14
  1215.0 170.5 all-reduce.13
  1388.6 27.6 reduce-scatter.16
  1421.2 119.4 all-reduce.11
where the time goes:
time: 1560 us; the launch traced here: 1550 us
  waiting for transfers between devices  1070 us (69%)
  matrix products  302 us (19%)
  other arithmetic  108 us (7%)
  local copies, waits for them, and re-layouts  56.9 us (4%)
  between operations  17.8 us (1%)
    all_gather x1, waiting for transfers between devices, shards(): lax.all_gather(gate_up_projection_weight, 'shard', axis=1, tiled=True)  308 us
    all_gather x1, waiting for transfers between devices, shards(): pieces = lax.all_gather(query_key_value_weight, 'shard', axis=1, tiled=True)  189 us
    unnamed x16, waiting for transfers between devices  153 us
    psum x1, waiting for transfers between devices, shards(): lax.psum(owned[0].astype(jnp.bfloat16), 'rep').astype(jnp.float32)  105 us
    all_gather x1, waiting for transfers between devices, shards(): lax.all_gather(down_projection_weight, 'shard', axis=0, tiled=True)  95.6 us
    reduce_scatter x1, waiting for transfers between devices, shards(): lax.psum_scatter(value_terms.astype(jnp.bfloat16), 'shard', scatter_dimen...  36.1 us
    all_gather x1, waiting for transfers between devices, shards(): lax.all_gather(value_low, 'shard', axis=0, tiled=True)  33.5 us
    all_gather x1, waiting for transfers between devices, shards(): lax.all_gather(key_turned, 'shard', axis=0, tiled=True)  33 us
  transfers between devices with their start and end apart: 15, of which 14 were waited for; matrix products, arithmetic and copies ran while one was open for 18% of the time, Pallas kernels for 0%

commit v1 on v0

--- a/solution.py
+++ b/solution.py
@@ -99,7 +99,15 @@
     b_hidden_one = lax.dynamic_index_in_dim(b_hidden_all, pick, 1, keepdims=False)
     normed = norm_rows(residual_in, gain_one).astype(jnp.bfloat16)
     empty = jnp.zeros((local_rows, width), jnp.float32)
-    pieces = lax.all_gather(query_key_value_weight, "shard", axis=1, tiled=True)
+    size = lax.axis_size("shard")
+    moving, blocks = (query_key_value_weight, [query_key_value_weight])
+    for _ in range(size - 1):
+        moving = lax.ppermute(moving, "shard", [(i, (i + 1) % size) for i in range(size)])
+        blocks.insert(0, moving)
+    merged = jnp.concatenate(blocks, axis=1)
+    pieces = jnp.roll(
+        merged, (lax.axis_index("shard") + 1) * query_key_value_weight.shape[1], axis=1
+    )
     columns = normed
     base_query, base_key, base_value = tuple(
         (jnp.dot(columns, pieces[slot], preferred_element_type=jnp.float32) for slot in range(3))

time: 1560 us -> 1870 us (1.20)
  waiting for transfers between devices: 1070 us -> 1320 us
  local copies, waits for them, and re-layouts: 56.9 us -> 107 us
    ppermute x0 -> x3, waiting for transfers between devices: none -> 255 us  [shards(): lax.ppermute(moving, 'shard', [(i, (i + 1) % size) for i in range(size)])]
    all_gather x1, waiting for transfers between devices: 95.6 us -> 157 us  [shards(): lax.all_gather(down_projection_weight, 'shard', axis=0, tiled=True)]
    unnamed x160 -> x163, local copies, waits for them, and re-layouts: 16.6 us -> 61.9 us
    all_gather x1, waiting for transfers between devices: 33.5 us -> 0.02 us  [shards(): lax.all_gather(value_low, 'shard', axis=0, tiled=True)]
    all_gather x1, waiting for transfers between devices: 29.6 us -> 0.01 us  [shards(): lax.all_gather(adapter_model_input_maps, 'shard', axis=1, tiled=True)]
  transfers between devices with their start and end apart: 15 -> 18, of which waited for: 14 -> 15; matrix products, arithmetic and copies ran while one was open for 18% -> 15% of each run, Pallas kernels for 0% -> 0%
where the time goes in v1:
time: 1870 us; the launch traced here: 1860 us
  waiting for transfers between devices  1320 us (71%)
  matrix products  309 us (17%)
  local copies, waits for them, and re-layouts  107 us (6%)
  other arithmetic  106 us (6%)
    all_gather x1, waiting for transfers between devices, shards(): lax.all_gather(gate_up_projection_weight, 'shard', axis=1, tiled=True)  310 us
    ppermute x3, waiting for transfers between devices, shards(): lax.ppermute(moving, 'shard', [(i, (i + 1) % size) for i in range(size)])  255 us
    all_gather x1, waiting for transfers between devices, shards(): lax.all_gather(query_key_value_weight, 'shard', axis=1, tiled=True)  193 us
    all_gather x1, waiting for transfers between devices, shards(): lax.all_gather(down_projection_weight, 'shard', axis=0, tiled=True)  157 us
    unnamed x16, waiting for transfers between devices  153 us
    psum x1, waiting for transfers between devices, shards(): lax.psum(owned[0].astype(jnp.bfloat16), 'rep').astype(jnp.float32)  103 us
    unnamed x163, local copies, waits for them, and re-layouts  61.9 us
  transfers between devices with their start and end apart: 18, of which 15 were waited for; matrix products, arithmetic and copies ran while one was open for 15% of the time, Pallas kernels for 0%

profile of v1, /device:TPU:0, one launch (start us, length us, event | category | flops | bytes accessed | tf_op | source)
XLA Modules:
  0.0 1863.7 jit_solution(6999120107989978421)
XLA Ops:
  7.7 88.8 %collective-permute-done = bf16[3,576,2304]{2,1,0:T(8,128)(2,1)} collective-permute-done((bf16[3,576,2304]{2,1,0:T(8,128)(2,1)}, bf16[3,576,2304]{2,1,0:T(8,128)(2,1)}, u32[]{:S(2)}, u32[]{:S(2)}) %collective-permute-start) | collective-permute-done | bytes 7962656 | tf_op jit(solution)/shard_map/ppermute | solution.py:105
  98.8 105.4 %collective-permute-done.1 = bf16[3,576,2304]{2,1,0:T(8,128)(2,1)} collective-permute-done((bf16[3,576,2304]{2,1,0:T(8,128)(2,1)}, bf16[3,576,2304]{2,1,0:T(8,128)(2,1)}, u32[]{:S(2)}, u32[]{:S(2)}) %collective-permute-start.1) | collective-permute-done | bytes 7962656 | tf_op jit(solution)/shard_map/ppermute | solution.py:105
  208.3 34.7 %all-gather.14.cloned.1.call-done = bf16[5,8,16,2304]{3,2,0,1:T(8,128)(2,1)} async-done(((bf16[5,2,16,2304]{3,2,0,1:T(8,128)(2,1)}), bf16[5,8,16,2304]{3,2,0,1:T(8,128)(2,1)}) %all-gather.14.cloned.1.call-update) | async-done | bytes 2949136 | tf_op jit(solution)/shard_map/all_gather | solution.py:92
  247.9 60.7 %collective-permute-done.2 = bf16[3,576,2304]{2,1,0:T(8,128)(2,1)} collective-permute-done((bf16[3,576,2304]{2,1,0:T(8,128)(2,1)}, bf16[3,576,2304]{2,1,0:T(8,128)(2,1)}, u32[]{:S(2)}, u32[]{:S(2)}) %collective-permute-start.2) | collective-permute-done | bytes 7962656 | tf_op jit(solution)/shard_map/ppermute | solution.py:105
  439.9 21.5 %all-gather.18.cloned.1.call-done = bf16[1024,2304]{1,0:T(8,128)(2,1)} async-done(((bf16[256,2304]{1,0:T(8,128)(2,1)}), bf16[1024,2304]{1,0:T(8,128)(2,1)}) %all-gather.18.cloned.1.call-update) | async-done | bytes 4718608 | tf_op jit(solution)/shard_map/all_gather | solution.py:127
  468.0 19.3 %fusion.6 = (f32[36,256]{1,0:T(8,128)S(1)}, f32[36,256,1024]{2,1,0:T(8,128)}) fusion(pred[256,1024]{1,0:T(8,128)(4,1)S(1)} %fusion.91, bf16[256,36,64]{0,2,1:T(8,128)(2,1)S(1)} %bitcast.305, bf16[1024,36,64]{0,2,1:T(8,128)(2,1)} %bitcast.298), kind=kOutput, calls=%fused_computation.11 | convolution fusion | flops 1236261888 | bytes 43945984 | tf_op jit(solution)/shard_map/qhd,khd->hqk/dot_general | solution.py:56
  487.3 17.5 fusion
  504.9 15.9 fusion.65
  545.2 17.5 all-gather.24.cloned.1.call-done
  569.6 157.1 %all-gather.26.cloned.1.call-done = bf16[5760,2304]{1,0:T(8,128)(2,1)} async-done(((bf16[1440,2304]{1,0:T(8,128)(2,1)}), bf16[5760,2304]{1,0:T(8,128)(2,1)}) %all-gather.26.cloned.1.call-update) | async-done | bytes 26542096 | tf_op jit(solution)/shard_map/all_gather | solution.py:177
  726.7 14.5 fusion.93
  752.8 309.9 %all-gather.22.cloned.1.call-done = bf16[2,2304,5760]{2,1,0:T(8,128)(2,1)} async-done(((bf16[2,576,5760]{2,1,0:T(8,128)(2,1)}), bf16[2,2304,5760]{2,1,0:T(8,128)(2,1)}) %all-gather.22.cloned.1.call-update) | async-done | bytes 53084176 | tf_op jit(solution)/shard_map/all_gather | solution.py:165
  1062.7 26.4 %convolution_bitcast_fusion = f32[2,256,5760]{2,1,0:T(8,128)} fusion(bf16[256,2304,1]{1,0,2:T(8,128)(2,1)S(1)} %fusion.66, bf16[2,2304,5760]{2,1,0:T(8,128)(2,1)} %all-gather.22.cloned.1.call-done), kind=kOutput, calls=%fused_computation.18 | convolution fusion | flops 13589544960 | bytes 66060288 | tf_op jit(solution)/shard_map/tr,srf->stf/dot_general | solution.py:162
  1110.8 23.9 %convolution_bitcast_fusion.2 = f32[256,2304]{1,0:T(8,128)} fusion(bf16[2,2304,5760]{2,1,0:T(8,128)(2,1)} %all-gather.22.cloned.1.call-done, bf16[1,256,5760]{2,1,0:T(8,128)(2,1)} %get-tuple-element.17, bf16[1,256,5760]{2,1,0:T(8,128)(2,1)} %get-tuple-element.13), kind=kOutput, calls=%fused_computation.52 | convolution fusion | flops 13592494080 | bytes 61341696 | tf_op jit(solution)/shard_map/stf,srf->tr/dot_general | solution.py:218
  1148.9 29.5 %multiply_reduce_fusion = (f32[36,256]{1,0:T(8,128)S(1)}, f32[36,256,1024]{2,1,0:T(8,128)}) fusion(f32[36,256]{1,0:T(8,128)S(1)} %copy-done.33, f32[36,256,1024]{2,1,0:T(8,128)} %get-tuple-element.40, pred[256,1024]{1,0:T(8,128)(4,1)S(1)} %copy-done.18, bf16[256,36,64]{0,2,1:T(8,128)(2,1)S(1)} %bitcast.317, bf16[1024,36,64]{0,2,1:T(8,128)(2,1)} %bitcast.302), kind=kOutput, calls=%fused_computation.1 | convolution fusion | flops 1255136256 | bytes 81731584 | tf_op jit(solution)/shard_map/qhd,khd->hqk/dot_general | solution.py:248
  1178.4 31.2 %multiply_convert_fusion = bf16[36,256,1024]{2,1,0:T(8,128)(2,1)} fusion(f32[36,256,1024]{2,1,0:T(8,128)} %get-tuple-element.46, f32[36,256]{1,0:T(8,128)S(1)} %get-tuple-element.45, f32[36,256]{1,0:T(8,128)S(1)} %copy-done.33, f32[36,256,1024]{2,1,0:T(8,128)} %get-tuple-element.40, pred[256,1024]{1,0:T(8,128)(4,1)S(1)} %copy-done.18), kind=kLoop, calls=%fused_computation | loop fusion | flops 56623104 | bytes 94707712 | tf_op jit(solution)/shard_map/convert_element_type | solution.py:252
  1221.6 21.0 %fusion.44 = bf16[36,64,1024]{2,1,0:T(8,128)(2,1)} fusion(bf16[256,36,64]{0,2,1:T(8,128)(2,1)S(1)} %bitcast.318, f32[36,256]{1,0:T(8,128)S(1)} %copy-done.33, f32[36,256,1024]{2,1,0:T(8,128)} %get-tuple-element.40, pred[256,1024]{1,0:T(8,128)(4,1)S(1)} %copy-done.18), kind=kOutput, calls=%fused_computation.89 | convolution fusion | flops 1248067584 | bytes 43945984 | tf_op jit(solution)/shard_map/hqk,qhd->khd/dot_general | solution.py:266
  1285.0 35.2 %reduce-scatter.15.cloned.1.call-done = bf16[256,2304]{1,0:T(8,128)(2,1)} async-done(((bf16[1024,2304]{1,0:T(8,128)(2,1)}), bf16[256,2304]{1,0:T(8,128)(2,1)}) %reduce-scatter.15.cloned.1.call-update) | async-done | bytes 1179664 | tf_op jit(solution)/shard_map/reduce_scatter | solution.py:276
  1337.2 13.5 fusion.150
  1353.2 149.0 %all-reduce.14.cloned.1.call-done = (bf16[6,8,16,2304]{3,2,1,0:T(8,128)(2,1)}, bf16[5,8,16,2304]{3,2,1,0:T(8,128)(2,1)}, bf16[2,8,16,5760]{3,2,1,0:T(8,128)(2,1)}) async-done(((bf16[6,8,16,2304]{3,2,1,0:T(8,128)(2,1)}, bf16[5,8,16,2304]{3,2,1,0:T(8,128)(2,1)}, bf16[2,8,16,5760]{3,2,1,0:T(8,128)(2,1)}), (bf16[6,8,16,2304]{3,2,1,0:T(8,128)(2,1)}, bf16[5,8,16,2304]{3,2,1,0:T(8,128)(2,1)}, ...) | async-done | bytes 9437200
  1508.4 24.6 %reduce-scatter.17.cloned.1.call-done = bf16[1,2,16,5760]{3,2,1,0:T(8,128)(2,1)} async-done(((bf16[1,8,16,5760]{3,2,1,0:T(8,128)(2,1)}), bf16[1,2,16,5760]{3,2,1,0:T(8,128)(2,1)}) %reduce-scatter.17.cloned.1.call-update) | async-done | bytes 368656 | tf_op jit(solution)/shard_map/reduce_scatter | solution.py:326
  1533.1 193.5 %all-gather.28.cloned.1.call-done = bf16[3,2304,2304]{2,1,0:T(8,128)(2,1)} async-done(((bf16[3,576,2304]{2,1,0:T(8,128)(2,1)}), bf16[3,2304,2304]{2,1,0:T(8,128)(2,1)}) %all-gather.28.cloned.1.call-update) | async-done | bytes 31850512 | tf_op jit(solution)/shard_map/all_gather | solution.py:300
  1726.5 17.0 convolution_bitcast_fusion.1
  1748.0 102.9 %all-reduce.12.cloned.1.call-done = (bf16[6,2,16,2304]{3,2,1,0:T(8,128)(2,1)}, bf16[5,2,16,2304]{3,2,1,0:T(8,128)(2,1)}, bf16[2,16,5760]{2,1,0:T(8,128)(2,1)}, bf16[2,2,16,5760]{3,2,1,0:T(8,128)(2,1)}) async-done(((bf16[6,2,16,2304]{3,2,1,0:T(8,128)(2,1)}, bf16[5,2,16,2304]{3,2,1,0:T(8,128)(2,1)}, bf16[2,16,5760]{2,1,0:T(8,128)(2,1)}, bf16[2,2,16,5760]{3,2,1,0:T(8,128)(2,1)}), ...) | async-done | bytes 2727952 | tf_op jit(solution)/shard_map/psum | solution.py:334
  (289 shorter events, 315.5 us)
Async XLA Ops:
  7.2 197.0 %copy-start.30 = (bf16[5,2,16,2304]{3,2,1,0:T(8,128)(2,1)S(1)}, bf16[5,2,16,2304]{3,2,1,0:T(8,128)(2,1)}, u32[]{:S(2)}) copy-start(bf16[5,2,16,2304]{3,2,1,0:T(8,128)(2,1)} %param.25) | copy-start | bytes 2211844
  7.2 198.6 %copy-start.62 = (bf16[2304]{0:T(1024)(128)(2,1)S(1)}, bf16[2304]{0:T(1024)(128)(2,1)}, u32[]{:S(2)}) copy-start(bf16[2304]{0:T(1024)(128)(2,1)} %param.18) | copy-start | bytes 13828
  7.2 198.7 %copy-start.9 = (bf16[1,256,2304]{2,1,0:T(8,128)(2,1)S(1)}, bf16[1,256,2304]{2,1,0:T(8,128)(2,1)}, u32[]{:S(2)}) copy-start(bf16[1,256,2304]{2,1,0:T(8,128)(2,1)} %param.14) | copy-start | bytes 3538948
  7.2 199.6 %all-gather.12.cloned.1.call-start = ((), (), s32[]{:S(2)}) async-start(), calls=%async_computation.3 | async-start | bytes 4423680 | tf_op jit(solution)/shard_map/all_gather | solution.py:91
  7.2 89.3 %collective-permute-start = (bf16[3,576,2304]{2,1,0:T(8,128)(2,1)}, bf16[3,576,2304]{2,1,0:T(8,128)(2,1)}, u32[]{:S(2)}, u32[]{:S(2)}) collective-permute-start(bf16[3,576,2304]{2,1,0:T(8,128)(2,1)} %param.20), channel_id=1, source_target_pairs={{0,1},{1,2},{2,3},{3,0},{4,5},{5,6},{6,7},{7,4},{8,9},{9,10},{10,1... | collective-permute-start | bytes 23887880 | tf_op jit(solution)/shard_map/ppermute | solution.py:105
  96.6 107.6 %collective-permute-start.1 = (bf16[3,576,2304]{2,1,0:T(8,128)(2,1)}, bf16[3,576,2304]{2,1,0:T(8,128)(2,1)}, u32[]{:S(2)}, u32[]{:S(2)}) collective-permute-start(bf16[3,576,2304]{2,1,0:T(8,128)(2,1)} %collective-permute-done), channel_id=1, source_target_pairs={{0,1},{1,2},{2,3},{3,0},{4,5},{5,6},{6,7},{7,4},{8,9},{9,10},{10,1... | collective-permute-start | bytes 23887880 | tf_op jit(solution)/shard_map/ppermute | solution.py:105
  98.7 144.3 %all-gather.14.cloned.1.call-start = ((), (), s32[]{:S(2)}) async-start(), calls=%async_computation.4 | async-start | bytes 3686400 | tf_op jit(solution)/shard_map/all_gather | solution.py:92
  204.1 104.4 %collective-permute-start.2 = (bf16[3,576,2304]{2,1,0:T(8,128)(2,1)}, bf16[3,576,2304]{2,1,0:T(8,128)(2,1)}, u32[]{:S(2)}, u32[]{:S(2)}) collective-permute-start(bf16[3,576,2304]{2,1,0:T(8,128)(2,1)} %collective-permute-done.1), channel_id=1, source_target_pairs={{0,1},{1,2},{2,3},{3,0},{4,5},{5,6},{6,7},{7,4},{8,9},{9,10},{10,1... | collective-permute-start | bytes 23887880 | tf_op jit(solution)/shard_map/ppermute | solution.py:105
  205.1 227.6 %all-gather.16.cloned.1.call-start = ((), (), s32[]{:S(2)}) async-start(), calls=%async_computation.5 | async-start | bytes 5898240 | tf_op jit(solution)/shard_map/all_gather | solution.py:128
  205.8 182.3 %copy-start.51 = (f32[2304]{0:T(1024)}, f32[2304]{0:T(1024)S(1)}, u32[]{:S(2)}) copy-start(f32[2304]{0:T(1024)S(1)} %convert_element_type.235) | copy-start | bytes 27652
  367.4 94.0 %all-gather.18.cloned.1.call-start = ((), (), s32[]{:S(2)}) async-start(), calls=%async_computation.6 | async-start | bytes 5898240 | tf_op jit(solution)/shard_map/all_gather | solution.py:127
  421.4 112.4 %all-gather.20.cloned.1.call-start = ((), (), s32[]{:S(2)}) async-start(), calls=%async_computation.7 | async-start | bytes 13271040 | tf_op jit(solution)/shard_map/all_gather | solution.py:146
  422.0 140.7 %all-gather.24.cloned.1.call-start = ((), (), s32[]{:S(2)}) async-start(), calls=%async_computation.9 | async-start | bytes 3686400 | tf_op jit(solution)/shard_map/all_gather | solution.py:94
  422.6 304.1 %all-gather.26.cloned.1.call-start = ((), (), s32[]{:S(2)}) async-start(), calls=%async_computation.10 | async-start | bytes 33177600 | tf_op jit(solution)/shard_map/all_gather | solution.py:177
  423.3 324.1 %all-gather.30.cloned.1.call-start = ((), (), s32[]{:S(2)}) async-start(), calls=%async_computation.15 | async-start | bytes 1843200 | tf_op jit(solution)/shard_map/all_gather | solution.py:93
  424.1 638.6 %all-gather.22.cloned.1.call-start = ((), (), s32[]{:S(2)}) async-start(), calls=%async_computation.8 | async-start | bytes 66355200 | tf_op jit(solution)/shard_map/all_gather | solution.py:165
  424.8 855.0 %reduce-scatter.13.cloned.1.call-start = ((), (), s32[]{:S(2)}) async-start(), calls=%async_computation.11 | async-start | bytes 5898240 | tf_op jit(solution)/shard_map/reduce_scatter | solution.py:273
  541.9 599.0 %copy-start.1 = (f32[256,2304]{1,0:T(8,128)}, f32[256,2304]{1,0:T(8,128)S(1)}, u32[]{:S(2)}) copy-start(f32[256,2304]{1,0:T(8,128)S(1)} %get-tuple-element.42) | copy-start | bytes 7077892
  542.9 519.7 %copy-start.13 = (bf16[256,2304,1]{1,0,2:T(8,128)(2,1)}, bf16[256,2304,1]{1,0,2:T(8,128)(2,1)S(1)}, u32[]{:S(2)}) copy-start(bf16[256,2304,1]{1,0,2:T(8,128)(2,1)S(1)} %fusion.66) | copy-start | bytes 3538948
  1221.6 98.6 %reduce-scatter.15.cloned.1.call-start = ((), (), s32[]{:S(2)}) async-start(), calls=%async_computation.12 | async-start | bytes 5898240 | tf_op jit(solution)/shard_map/reduce_scatter | solution.py:276
  1249.3 252.9 %all-reduce.14.cloned.1.call-start = ((), (), s32[]{:S(2)}) async-start(), calls=%async_computation.17 | async-start | bytes 18874368
  1331.5 201.6 %reduce-scatter.17.cloned.1.call-start = ((), (), s32[]{:S(2)}) async-start(), calls=%async_computation.14 | async-start | bytes 1843200 | tf_op jit(solution)/shard_map/reduce_scatter | solution.py:326
  1335.2 391.3 %all-gather.28.cloned.1.call-start = ((), (), s32[]{:S(2)}) async-start(), calls=%async_computation.13 | async-start | bytes 39813120 | tf_op jit(solution)/shard_map/all_gather | solution.py:300
  1335.8 515.1 %all-reduce.12.cloned.1.call-start = ((), (), s32[]{:S(2)}) async-start(), calls=%async_computation.16 | async-start | bytes 5455872 | tf_op jit(solution)/shard_map/psum | solution.py:334
  (69 other events, 740.9 us)
Sparse Core Ops, SparseCore 0:
  98.8 42.6 all-gather.11
  205.2 37.7 all-gather.13
  367.5 39.5 all-gather.15
  421.5 39.8 all-gather.17
  462.8 70.9 all-gather.19
  535.2 27.4 all-gather.23
  564.2 162.4 all-gather.25
  728.2 19.0 all-gather.29
  749.0 313.6 all-gather.21
  1221.7 47.8 reduce-scatter.12
  1272.2 47.8 reduce-scatter.14
  1331.6 170.5 all-reduce.13
  1505.3 27.6 reduce-scatter.16
  1534.5 191.9 all-gather.27
  1731.4 119.4 all-reduce.11
